TPU v7x, 32 devices: a whole 2x2x4 slice. The times are simulated.
32 devices in a mesh: row: 8 (over y, x, core), col: 4 (over z).
Axes of the slice: x: 2, y: 2, z: 4, core: 2. Of those that a mesh axis runs over, the one named last changes fastest.
Arguments:
- vector: float32 [4096, 4096], P('row', 'col'), may hold values from -6 to 6
- one_electron: float32 [16, 16], replicated, may hold values from -0.18 to 0.18
- links: int32 [32, 8], replicated, may hold values from 0 to 31, as said below
- counts: int32 [32], replicated, may hold values from 4 to 8, as said below
- pairs: int32 [32, 8], P('row'), may hold values from 0 to 255
- signs: int32 [32, 8, 128, 128], P('row'), may hold values from -1 to 1
Outputs:
- sigma_vector: float32 [4096, 4096], P('row', 'col')
Inputs may be any that keep to these rules, and one draw needn't show every extreme that they name: `links`: entries name string blocks; only the first counts[I] entries of block I are used. Counting used entries only, the blocks I with I // 4 = d name blocks K with K // 4 = s at most 4 times for any d and s, and some pair d, s reaches 4. Block I has counts[I] used links; every block I with I % 4 = 0 has 8.
All inputs are finite; a program needn't handle non-finite values.
Results may differ from a plain program's by a relative error of at most 0.000051.
Values sent between devices are 32-bit elements; how exact they have to be, the bound alone decides.
A program may use at most 128 MiB of HBM per device.

v0:
```python
import jax
import jax.numpy as jnp
from jax import lax
from jax.sharding import PartitionSpec as P


def broadcast(value, axis, source):
    kept = jnp.where(lax.axis_index(axis) == source, value, 0).astype(value.dtype)
    return lax.psum(kept, axis)


def pair_values(pair_ids, used, integrals):
    flat_table = integrals.reshape(-1)
    onehot = pair_ids[:, :, None] == jnp.arange(flat_table.shape[0], dtype=jnp.int32)[None, None, :]
    values = jnp.sum(jnp.where(onehot, flat_table[None, None, :], 0.0), axis=2)
    in_use = jnp.arange(pair_ids.shape[1], dtype=jnp.int32)[None, :] < used[:, None]
    return jnp.where(in_use, values, 0.0)


def local(vector, one_electron, links, counts, pairs, signs):
    block_size = signs.shape[2]
    blocks_a = pairs.shape[0]
    link_max = links.shape[1]
    rows_here, cols_here = vector.shape
    row_count = lax.axis_size("row")
    col_count = lax.axis_size("col")
    row_index = lax.axis_index("row")
    col_index = lax.axis_index("col")
    spread = row_count // col_count
    blocks_b = blocks_a * spread
    local_counts_a = lax.dynamic_slice_in_dim(counts, row_index * blocks_a, blocks_a)
    replace_alpha = pair_values(pairs, local_counts_a, one_electron)[
        :, :, None, None
    ] * signs.astype(jnp.float32)
    whole_column = lax.all_gather(vector, "row", axis=0, tiled=True).reshape(
        -1, block_size, cols_here
    )
    local_links_a = lax.dynamic_slice_in_dim(links, row_index * blocks_a, blocks_a)
    fetched_alpha = whole_column[local_links_a.reshape(-1)]
    fetched_alpha = fetched_alpha.reshape(blocks_a, link_max, block_size, cols_here)
    sigma_alpha = jnp.einsum(
        "ilmk,ilkw->imw", replace_alpha, fetched_alpha, precision=lax.Precision.HIGHEST
    )
    sigma_alpha = sigma_alpha.reshape(rows_here, cols_here)
    table_pieces = []
    for offset in range(spread):
        owner = col_index * spread + offset
        table_pieces.append(broadcast(replace_alpha, "row", owner))
    replace_beta = jnp.concatenate(table_pieces, axis=0)
    whole_row = lax.all_gather(vector, "col", axis=1, tiled=True).reshape(rows_here, -1, block_size)
    local_links_b = lax.dynamic_slice_in_dim(links, col_index * blocks_b, blocks_b)
    fetched_beta = jnp.take(whole_row, local_links_b.reshape(-1), axis=1)
    fetched_beta = fetched_beta.reshape(rows_here, blocks_b, link_max, block_size)
    sigma_beta = jnp.einsum(
        "rjlk,jlmk->rjm", fetched_beta, replace_beta, precision=lax.Precision.HIGHEST
    )
    sigma_beta = sigma_beta.reshape(rows_here, cols_here)
    return sigma_alpha + sigma_beta


def solution(mesh):
    in_specs = (P("row", "col"), P(), P(), P(), P("row", None), P("row", None, None, None))
    out_specs = P("row", "col")
    return jax.shard_map(local, mesh=mesh, in_specs=in_specs, out_specs=out_specs, check_vma=False)
```

profile of v0, /device:TPU:4, one launch (start us, length us, event | category | flops | bytes accessed | tf_op | source)
XLA Modules:
  0.0 285.7 jit_solution(3965529795193562592)
XLA Ops:
  7.4 0.0 all-gather.5.cloned.1.call-start
  7.4 2.9 %copy.24 = f32[512,1024]{0,1:T(8,128)} copy(f32[512,1024]{1,0:T(8,128)} %param.6) | data formatting | bytes 4194304 | tf_op args[0]
  10.2 0.0 copy-start.3
  10.3 0.0 copy-start.5
  10.3 0.0 copy-start.4
  10.3 0.0 copy-start
  10.3 0.0 all-gather.5.cloned.1.call-update
  10.3 0.0 all-reduce.3.cloned.1.call-start
  10.4 0.6 copy-done.3
  10.9 0.1 broadcast_in_dim.39
  11.0 0.0 copy-done.5
  11.0 0.1 dynamic_slice.9
  11.1 0.0 copy-done.4
  11.1 0.2 select_reduce_fusion
  11.3 0.1 fusion.11
  11.3 0.6 copy-done
  11.9 2.3 fusion.8
  14.2 0.0 all-reduce.3.cloned.1.call-update
  14.2 0.0 copy-start.2
  14.2 0.0 all-gather.3.cloned.1.call-start
  14.2 0.7 all-gather.3.cloned.1.call-update
  14.9 0.0 copy-done.2
  15.0 0.1 constant_dynamic-slice_fusion.1
  15.0 0.1 copy.22
  15.1 0.1 reshape.113
  15.2 0.1 compare_and_fusion
  15.3 0.1 copy.23
  15.4 0.1 copy.25
  15.4 0.1 reshape.117
  15.6 145.7 %all-gather.5.cloned.1.call-done = f32[512,4096]{0,1:T(8,128)} async-done(((f32[512,1024]{0,1:T(8,128)}), f32[512,4096]{0,1:T(8,128)}) %all-gather.5.cloned.1.call-update) | async-done | bytes 8388624 | tf_op jit(solution)/shard_map/all_gather | solution.py:50
  161.3 9.2 %copy.26 = f32[512,32,128]{2,0,1:T(8,128)} copy(f32[512,32,128]{0,2,1:T(8,128)} %bitcast.26) | data formatting | bytes 16777216 | tf_op jit(solution)/shard_map/reshape | solution.py:50
  170.4 13.1 %gather_fusion.1 = f32[64,512,128]{2,1,0:T(8,128)} fusion(f32[512,32,128]{2,0,1:T(8,128)} %copy.26, s32[1024]{0:T(1024)S(1)} %pad_clamp_fusion), kind=kCustom, calls=%fused_computation.1 | custom fusion | bytes 33554688 | tf_op jit(solution)/shard_map/jit(_take)/gather | solution.py:52
  183.6 0.0 all-reduce.3.cloned.1.call-done
  183.6 23.0 %fusion = f32[8,128,512,1]{2,1,3,0:T(8,128)} fusion(f32[512,8,8,128]{3,0,2,1:T(8,128)} %bitcast.22, pred[8,8]{1,0:T(8,128)(4,1)S(1)} %copy.23, f32[4,8,128,128]{3,2,1,0:T(8,128)} %get-tuple-element.5, f32[4,8,128,128]{3,2,1,0:T(8,128)} %get-tuple-element.6), kind=kOutput, calls=%fused_computation.2 | convolution fusion | flops 6447693824 | bytes 23068736 | tf_op jit(solution)/shard_map/rjlk,jlmk->rjm/dot_general | solution.py:54
  206.5 2.9 %copy.27 = f32[512,1024]{1,0:T(8,128)} copy(f32[512,1024]{0,1:T(8,128)} %bitcast.25) | data formatting | bytes 4194304 | tf_op jit(solution)/shard_map/reshape | solution.py:57
  209.4 40.9 %all-gather.3.cloned.1.call-done = f32[4096,1024]{1,0:T(8,128)} async-done(((f32[512,1024]{1,0:T(8,128)}), f32[4096,1024]{1,0:T(8,128)}) %all-gather.3.cloned.1.call-update) | async-done | bytes 16777232 | tf_op jit(solution)/shard_map/all_gather | solution.py:35
  250.4 14.1 %gather_fusion = f32[32,128,1024]{2,1,0:T(8,128)} fusion(f32[32,128,1024]{2,1,0:T(8,128)} %bitcast.24, s32[1024]{0:T(1024)S(1)} %pad_clamp_fusion.1), kind=kCustom, calls=%fused_computation | custom fusion | bytes 33554560 | tf_op jit(solution)/shard_map/gather | solution.py:39
  264.5 0.0 copy-start.1
  264.5 12.1 %fusion.9 = f32[4,128,1024,1]{2,1,3,0:T(8,128)S(1)} fusion(f32[4,8,128,1024]{3,2,1,0:T(8,128)} %bitcast.23, s32[4,8,128,128]{3,2,1,0:T(8,128)S(1)} %copy-done, f32[4,8]{1,0:T(4,128)S(1)} %fusion.11), kind=kOutput, calls=%fused_computation.13 | convolution fusion | flops 6443499520 | bytes 20971648 | tf_op jit(solution)/shard_map/ilmk,ilkw->imw/dot_general | solution.py:41
  276.6 0.0 copy-done.1
  276.6 1.7 bitcast_add_fusion
  (4 shorter events, 0.0 us)
Async XLA Ops:
  7.4 153.9 %all-gather.5.cloned.1.call-start = ((), (), s32[]{:S(2)}) async-start(), calls=%async_computation.1 | async-start | bytes 10485760 | tf_op jit(solution)/shard_map/all_gather | solution.py:50
  10.2 0.7 copy-start.3
  10.3 0.8 copy-start.5
  10.3 0.9 copy-start.4
  10.3 1.6 copy-start
  10.3 173.3 %all-reduce.3.cloned.1.call-start = ((), (), s32[]{:S(2)}) async-start(), calls=%async_computation.2 | async-start | bytes 8388608 | tf_op jit(solution)/shard_map/psum | solution.py:9
  14.2 0.8 copy-start.2
  14.2 236.2 %all-gather.3.cloned.1.call-start = ((), (), s32[]{:S(2)}) async-start(), calls=%async_computation | async-start | bytes 18874368 | tf_op jit(solution)/shard_map/all_gather | solution.py:35
  264.5 12.1 %copy-start.1 = (f32[512,1024]{1,0:T(8,128)S(1)}, f32[512,1024]{1,0:T(8,128)}, u32[]{:S(2)}) copy-start(f32[512,1024]{1,0:T(8,128)} %copy.27) | copy-start | bytes 6291460
Sparse Core Ops, SparseCore 0:
  10.4 150.8 all-gather.4
  163.1 87.1 all-gather.2
Sparse Core Ops, SparseCore 1:
  14.3 81.6 all-reduce.2
where the time goes:
time: 288 us; the launch traced here: 286 us
  waiting for transfers between devices  187 us (65%)
  local copies, waits for them, and re-layouts  44 us (15%)
  matrix products  35.1 us (12%)
  between operations  14.9 us (5%)
  other arithmetic  4.33 us (2%)
    all_gather x1, waiting for transfers between devices, local(): lax.all_gather(vector, 'col', axis=1, tiled=True)  146 us
    all_gather x1, waiting for transfers between devices, local(): lax.all_gather(vector, 'row', axis=0, tiled=True)  40.9 us
    dot_general x1, matrix products, local(): jnp.einsum('rjlk,jlmk->rjm', fetched_beta, replace_beta, precision=lax.Pr...  23 us
    gather x1, local copies, waits for them, and re-layouts, local(): fetched_alpha = whole_column[local_links_a.reshape(-1)]  14.1 us
    gather x1, local copies, waits for them, and re-layouts, local(): fetched_beta = jnp.take(whole_row, local_links_b.reshape(-1), axis=1)  13.1 us
    dot_general x1, matrix products, local(): jnp.einsum('ilmk,ilkw->imw', replace_alpha, fetched_alpha, precision=lax....  12.1 us
    reshape x1, local copies, waits for them, and re-layouts, local(): lax.all_gather(vector, 'col', axis=1, tiled=True)  9.16 us
  transfers between devices with their start and end apart: 3, of which 2 were waited for; matrix products, arithmetic and copies ran while one was open for 18% of the time, Pallas kernels for 0%

commit v1 on v0

v1 whole, which is shorter than its diff:
```python
import functools

import jax
import jax.numpy as jnp
from jax import lax
from jax.experimental import pallas as pl
from jax.experimental.pallas import tpu as pltpu
from jax.sharding import PartitionSpec as P

MESH = pl.DeviceIdType.MESH
PARTS_A = 4
PARTS_B = 4
PAD = 8


def pair_values(pair_ids, used, integrals):
    flat_table = integrals.reshape(-1)
    onehot = pair_ids[:, :, None] == jnp.arange(flat_table.shape[0], dtype=jnp.int32)[None, None, :]
    values = jnp.sum(jnp.where(onehot, flat_table[None, None, :], 0.0), axis=2)
    in_use = jnp.arange(pair_ids.shape[1], dtype=jnp.int32)[None, :] < used[:, None]
    return jnp.where(in_use, values, 0.0)


def split(value):
    high = value.astype(jnp.bfloat16)
    low = (value - high.astype(jnp.float32)).astype(jnp.bfloat16)
    return high, low


def kernel(rows, cols, blocks, link_max, links, v, tab, out, *scratch):
    scratch = list(scratch)
    colbuf = [scratch.pop(0) for _ in range(PARTS_A)]
    rowbuf = [scratch.pop(0) for _ in range(PARTS_B)]
    own_tab, beta_tab, alpha_signs, beta_signs = scratch[:4]
    asend, arecv, bsend, brecv, tsend, trecv, lsem = scratch[4:]

    size = own_tab.shape[2]
    width = out.shape[1]
    wide = width // PARTS_A
    tall = out.shape[0] // PARTS_B
    spread = rows // cols
    blocks_b = blocks * spread
    tables = blocks * link_max
    chips = rows // 2
    reach = chips // 2
    across = chips // 2

    r = lax.axis_index("row")
    c = lax.axis_index("col")
    core = lax.rem(r, 2)
    chip = r // 2
    other = r + 1 - 2 * core
    place = jnp.where(chip < across, chip, chips - 1 - (chip - across))

    def chip_at(position):
        position = lax.rem(position + 2 * chips, chips)
        return jnp.where(position < across, position, across + (chips - 1 - position))

    def row_at(position, k):
        return 2 * chip_at(position) + k

    right = (row_at(place + 1, core), c)
    left = (row_at(place - 1, core), c)
    partner = (other, c)
    up = (r, jnp.minimum(c + 1, cols - 1))
    down = (r, jnp.maximum(c - 1, 0))
    has_up = c < cols - 1
    has_down = c > 0

    barrier = pltpu.get_barrier_semaphore()
    for device in (right, left, partner):
        pl.semaphore_signal(barrier, inc=1, device_id=device, device_id_type=MESH)

    @pl.when(has_up)
    def _():
        pl.semaphore_signal(barrier, inc=1, device_id=up, device_id_type=MESH)

    @pl.when(has_down)
    def _():
        pl.semaphore_signal(barrier, inc=1, device_id=down, device_id_type=MESH)

    loads = []
    for j in range(PARTS_A):
        for i in range(blocks):
            loads.append(pltpu.make_async_copy(
                v.at[pl.ds(i * size, size), pl.ds(j * wide, wide)],
                colbuf[j].at[r * blocks + i], lsem.at[len(loads)]))
    for i in range(PARTS_B):
        for k in range(blocks_b):
            loads.append(pltpu.make_async_copy(
                v.at[pl.ds(i * tall, tall), pl.ds(k * size, size)],
                rowbuf[i].at[c * blocks_b + k], lsem.at[len(loads)]))
    loads.append(pltpu.make_async_copy(tab, own_tab, lsem.at[len(loads)]))
    for load in loads:
        load.start()
    for load in loads:
        load.wait()

    pl.semaphore_wait(barrier, 3 + has_up.astype(jnp.int32) + has_down.astype(jnp.int32))

    pending = []

    def send(src, dst, ssem, rsem, device, cond=None):
        copy = pltpu.make_async_remote_copy(
            src_ref=src, dst_ref=dst, send_sem=ssem, recv_sem=rsem,
            device_id=device, device_id_type=MESH)
        pending.append((cond, copy))
        if cond is None:
            copy.start()
        else:
            pl.when(cond)(copy.start)

    def arrive(ref, ssem, rsem, cond=None):
        copy = pltpu.make_async_remote_copy(
            src_ref=ref, dst_ref=ref, send_sem=ssem, recv_sem=rsem,
            device_id=partner, device_id_type=MESH)
        if cond is None:
            copy.wait_recv()
        else:
            pl.when(cond)(copy.wait_recv)

    def alpha_part(j, position, k, t, leftward):
        start = row_at(position, k) * blocks
        count = blocks
        if t == reach - 1:
            count = blocks // 2
            if leftward:
                start = start + count
        return colbuf[j].at[pl.ds(start, count)]

    def alpha_send(j, t):
        ref = alpha_part(j, place - t, core, t, False)
        send(ref, ref, asend.at[j, t], arecv.at[j, t], right)
        ref = alpha_part(j, place + t, core, t, True)
        send(ref, ref, asend.at[j, reach + t], arecv.at[j, reach + t], left)

    def alpha_arrive(j, t):
        m = chips + 1 + t
        ref = alpha_part(j, place - 1 - t, core, t, False)
        arrive(ref, asend.at[j, t], arecv.at[j, t])
        send(ref, ref, asend.at[j, m], arecv.at[j, m], partner)
        m = m + reach
        ref = alpha_part(j, place + 1 + t, core, t, True)
        arrive(ref, asend.at[j, reach + t], arecv.at[j, reach + t])
        send(ref, ref, asend.at[j, m], arecv.at[j, m], partner)

    def alpha_partner(j):
        m = chips
        ref = colbuf[j].at[pl.ds(other * blocks, blocks)]
        arrive(ref, asend.at[j, m], arecv.at[j, m])
        for t in range(reach):
            m = chips + 1 + t
            arrive(alpha_part(j, place - 1 - t, 1 - core, t, False), asend.at[j, m], arecv.at[j, m])
            m = m + reach
            arrive(alpha_part(j, place + 1 + t, 1 - core, t, True), asend.at[j, m], arecv.at[j, m])

    def beta_part(i, tile):
        return rowbuf[i].at[pl.ds(jnp.clip(tile, 0, cols - 1) * blocks_b, blocks_b)]

    def beta_send(i, t):
        ref = beta_part(i, c - t)
        send(ref, ref, bsend.at[i, t], brecv.at[i, t], up, has_up & (c - t >= 0))
        ref = beta_part(i, c + t)
        m = cols - 1 + t
        send(ref, ref, bsend.at[i, m], brecv.at[i, m], down, has_down & (c + t < cols))

    def beta_arrive(i, t):
        arrive(beta_part(i, c - 1 - t), bsend.at[i, t], brecv.at[i, t], c - 1 - t >= 0)
        m = cols - 1 + t
        arrive(beta_part(i, c + 1 + t), bsend.at[i, m], brecv.at[i, m], c + 1 + t < cols)

    half = tables // 2

    def table_places(s):
        source = c * spread + s
        source_chip = source // 2
        source_place = jnp.where(
            source_chip < across, source_chip, chips - 1 - (source_chip - across))
        distance = lax.rem(place - source_place + chips, chips)
        return lax.rem(source, 2), distance

    def table_stage(s, first):
        source_core, distance = table_places(s)
        mine = core == source_core
        back = lax.rem(chips - distance, chips)
        at_source = mine & (distance == 0)
        for h in range(2):
            ref = beta_tab.at[s, pl.ds(h * half, half)]
            if first:
                here = at_source
                src = own_tab.at[pl.ds(h * half, half)]
            else:
                here = mine & (distance != 0)
                src = ref
                arrive(ref, tsend.at[s, h, 0], trecv.at[s, h], here)
            limit = reach if h == 0 else reach - 1
            other_limit = reach - 1 if h == 0 else reach
            go_right = here & (distance + 1 <= limit)
            go_left = here & (back + 1 <= other_limit)
            base = 0 if first else 3
            send(src, ref, tsend.at[s, h, base], trecv.at[s, h], right, go_right)
            send(src, ref, tsend.at[s, h, base + 1], trecv.at[s, h], left, go_left)
            send(src, ref, tsend.at[s, h, base + 2], trecv.at[s, h], partner, here)

    def table_finish(s):
        source_core, distance = table_places(s)
        mine = core == source_core
        for h in range(2):
            ref = beta_tab.at[s, pl.ds(h * half, half)]
            arrive(ref, tsend.at[s, h, 0], trecv.at[s, h], jnp.logical_not(mine))

    for j in range(PARTS_A):
        alpha_send(j, 0)
        ref = colbuf[j].at[pl.ds(r * blocks, blocks)]
        send(ref, ref, asend.at[j, chips], arecv.at[j, chips], partner)
        if j < PARTS_B:
            beta_send(j, 0)
    for i in range(PARTS_A, PARTS_B):
        beta_send(i, 0)
    for s in range(spread):
        table_stage(s, True)

    @pl.loop(0, tables)
    def _(index):
        signs = own_tab[index, :size, :].astype(jnp.bfloat16)
        alpha_signs[index] = jnp.concatenate([signs, signs], axis=1)

    def alpha_compute(j):
        @pl.loop(0, blocks)
        def _(block):
            total = jnp.zeros((size, wide), jnp.float32)
            for l in range(link_max):
                source = links[r * blocks + block, l]
                high, low = split(colbuf[j][source])
                index = block * link_max + l
                term = jnp.dot(alpha_signs[index], jnp.concatenate([high, low], axis=0),
                               preferred_element_type=jnp.float32)
                scale = own_tab[index, pl.ds(size, 1), :]
                scale = jnp.concatenate([scale] * (wide // size), axis=1)
                total = total + term * scale
            out[pl.ds(pl.multiple_of(block * size, size), size), pl.ds(j * wide, wide)] = total

    def beta_compute(i):
        @pl.loop(0, blocks_b)
        def _(block):
            total = jnp.zeros((tall, size), jnp.float32)
            for l in range(link_max):
                source = links[c * blocks_b + block, l]
                high, low = split(rowbuf[i][source])
                index = block * link_max + l
                term = lax.dot_general(
                    jnp.concatenate([high, low], axis=1), beta_signs[index],
                    (((1,), (1,)), ((), ())), preferred_element_type=jnp.float32)
                scale = beta_tab[block // blocks, lax.rem(index, tables), pl.ds(size, 1), :]
                total = total + term * scale
            where = (pl.ds(i * tall, tall), pl.ds(pl.multiple_of(block * size, size), size))
            out[where] = out[where] + total

    for t in range(1, max(reach, cols - 1) + 1):
        for j in range(max(PARTS_A, PARTS_B)):
            if j < PARTS_A and t <= reach:
                alpha_arrive(j, t - 1)
                if t < reach:
                    alpha_send(j, t)
            if j < PARTS_B and t < cols - 1:
                beta_arrive(j, t - 1)
                beta_send(j, t)
            if t == 1 and j == PARTS_A - 1:
                for s in range(spread):
                    table_stage(s, False)
            if t == reach and j < PARTS_A:
                if j > 0:
                    alpha_partner(j - 1)
                    alpha_compute(j - 1)
        if t == reach:
            alpha_partner(PARTS_A - 1)
            alpha_compute(PARTS_A - 1)
            for s in range(spread):
                source_core, distance = table_places(s)

                @pl.when((core == source_core) & (distance == 0))
                def _():
                    copy = pltpu.make_async_copy(own_tab, beta_tab.at[s], lsem.at[0])
                    copy.start()
                    copy.wait()

                table_finish(s)

                @pl.loop(0, tables)
                def _(index):
                    signs = beta_tab[s, index, :size, :].astype(jnp.bfloat16)
                    beta_signs[s * tables + index] = jnp.concatenate([signs, signs], axis=1)

    for i in range(PARTS_B):
        beta_arrive(i, cols - 2)
        beta_compute(i)

    for cond, copy in pending:
        if cond is None:
            copy.wait_send()
        else:
            pl.when(cond)(copy.wait_send)


def local(vector, one_electron, links, counts, pairs, signs, rows, cols):
    blocks, link_max = pairs.shape
    size = signs.shape[2]
    high, width = vector.shape
    spread = rows // cols
    tables = blocks * link_max
    used = lax.dynamic_slice_in_dim(counts, lax.axis_index("row") * blocks, blocks)
    coef = pair_values(pairs, used, one_electron).reshape(tables, 1, 1)
    tab = jnp.concatenate(
        [signs.reshape(tables, size, size).astype(jnp.float32),
         jnp.broadcast_to(coef, (tables, PAD, size))], axis=1)
    chips = rows // 2
    scratch = [pltpu.VMEM((rows * blocks, size, width // PARTS_A), jnp.float32)] * PARTS_A
    scratch += [pltpu.VMEM((cols * blocks * spread, high // PARTS_B, size), jnp.float32)] * PARTS_B
    scratch += [
        pltpu.VMEM((tables, size + PAD, size), jnp.float32),
        pltpu.VMEM((spread, tables, size + PAD, size), jnp.float32),
        pltpu.VMEM((tables, size, 2 * size), jnp.bfloat16),
        pltpu.VMEM((spread * tables, size, 2 * size), jnp.bfloat16),
        pltpu.SemaphoreType.DMA((PARTS_A, 2 * chips + 1)),
        pltpu.SemaphoreType.DMA((PARTS_A, 2 * chips + 1)),
        pltpu.SemaphoreType.DMA((PARTS_B, 2 * cols - 2)),
        pltpu.SemaphoreType.DMA((PARTS_B, 2 * cols - 2)),
        pltpu.SemaphoreType.DMA((spread, 2, 6)),
        pltpu.SemaphoreType.DMA((spread, 2)),
        pltpu.SemaphoreType.DMA((PARTS_A * blocks + PARTS_B * blocks * spread + 1,)),
    ]
    return pl.pallas_call(
        functools.partial(kernel, rows, cols, blocks, link_max),
        out_shape=jax.ShapeDtypeStruct(vector.shape, jnp.float32),
        in_specs=[
            pl.BlockSpec(memory_space=pltpu.SMEM),
            pl.BlockSpec(memory_space=pl.ANY),
            pl.BlockSpec(memory_space=pl.ANY),
        ],
        out_specs=pl.BlockSpec(memory_space=pltpu.VMEM),
        scratch_shapes=scratch,
        compiler_params=pltpu.CompilerParams(
            collective_id=0, has_side_effects=True, vmem_limit_bytes=60 << 20),
    )(links, vector, tab)


def solution(mesh):
    in_specs = (P("row", "col"), P(), P(), P(), P("row", None), P("row", None, None, None))
    out_specs = P("row", "col")
    body = functools.partial(local, rows=mesh.shape["row"], cols=mesh.shape["col"])
    return jax.shard_map(body, mesh=mesh, in_specs=in_specs, out_specs=out_specs, check_vma=False)
```

time: 288 us -> 184 us (0.64)
  waiting for transfers between devices: 187 us -> 0 us
  Pallas kernels: 0 us -> 174 us
  local copies, waits for them, and re-layouts: 44 us -> 5.53 us
  matrix products: 35.1 us -> 0 us
  between operations: 14.9 us -> 0.04 us
    all_gather x2 -> x0, waiting for transfers between devices: 187 us -> none  [the longest x1 146 us: local(): lax.all_gather(vector, 'col', axis=1, tiled=True)]
    pallas_call x0 -> x1, Pallas kernels: none -> 174 us  [local(): pl.pallas_call(functools.partial(kernel, rows, cols, blocks, link_max), o...]
    dot_general x2 -> x0, matrix products: 35.1 us -> none  [the longest x1 23 us: local(): jnp.einsum('rjlk,jlmk->rjm', fetched_beta, replace_beta, precision=lax.Pr...]
    gather x2 -> x0, local copies, waits for them, and re-layouts: 27.2 us -> none  [the longest x1 14.1 us: local(): fetched_alpha = whole_column[local_links_a.reshape(-1)]]
    reshape x4 -> x0, local copies, waits for them, and re-layouts: 12.2 us -> none  [the longest x1 9.16 us: local(): lax.all_gather(vector, 'col', axis=1, tiled=True)]
  transfers between devices with their start and end apart: 3 -> 0, of which waited for: 2 -> 0; matrix products, arithmetic and copies ran while one was open for 18% -> 0% of each run, Pallas kernels for 0% -> 0%
where the time goes in v1:
time: 184 us
  Pallas kernels  174 us (95%)
  local copies, waits for them, and re-layouts  5.53 us (3%)
  other arithmetic  4.21 us (2%)
    pallas_call x1, Pallas kernels, local(): pl.pallas_call(functools.partial(kernel, rows, cols, blocks, link_max), o...  174 us
    unnamed x4, local copies, waits for them, and re-layouts  3.85 us

profile of v1, /device:TPU:4, one launch (start us, length us, event | category | flops | bytes accessed | tf_op | source)
XLA Modules:
  0.0 184.1 jit_solution(3969349579743708943)
XLA Ops:
  0.0 0.7 dynamic_slice.3
  0.7 0.8 broadcast_in_dim.27
  1.5 0.8 select_reduce_fusion
  2.3 0.1 fusion
  2.4 0.1 select_n.21
  2.5 0.1 broadcast_in_dim.31
  2.6 1.7 convert_element_type.6
  4.3 0.0 copy-start
  4.4 1.6 pad_maximum_fusion.tab
  5.9 0.0 copy-done
  5.9 0.7 copy.8.links
  6.6 174.3 %shard_map.64 = f32[512,1024]{1,0:T(8,128)} custom-call(s32[32,8]{1,0:T(8,128)} %copy.8.links, f32[512,1024]{1,0:T(8,128)} %v.1, f32[32,136,128]{2,1,0:T(8,128)} %pad_maximum_fusion.tab), custom_call_target="tpu_custom_call" | custom-call | tf_op jit(solution)/shard_map/pallas_call | solution.py:332
  180.9 3.2 %copy.10 = f32[512,1024]{1,0:T(8,128)} copy(f32[512,1024]{1,0:T(8,128)} %shard_map.64) | data formatting | bytes 4194304
Async XLA Ops:
  4.3 1.6 copy-start

commit v2 on v1

--- a/solution.py
+++ b/solution.py
@@ -11,6 +11,7 @@
 PARTS_A = 4
 PARTS_B = 4
 PAD = 8
+PIECES = 4
 
 
 def pair_values(pair_ids, used, integrals):
@@ -31,8 +32,8 @@
     scratch = list(scratch)
     colbuf = [scratch.pop(0) for _ in range(PARTS_A)]
     rowbuf = [scratch.pop(0) for _ in range(PARTS_B)]
-    own_tab, beta_tab, alpha_signs, beta_signs = scratch[:4]
-    asend, arecv, bsend, brecv, tsend, trecv, lsem = scratch[4:]
+    own_tab, beta_tab, help_tab, alpha_signs, beta_signs, help_signs, shared = scratch[:7]
+    asend, arecv, bsend, brecv, tsend, trecv, hsend, hrecv, rsend, rrecv, lsem = scratch[7:]
 
     size = own_tab.shape[2]
     width = out.shape[1]
@@ -44,6 +45,7 @@
     chips = rows // 2
     reach = chips // 2
     across = chips // 2
+    helped = PARTS_B // 2 if cols >= 4 else 0
 
     r = lax.axis_index("row")
     c = lax.axis_index("col")
@@ -66,6 +68,11 @@
     down = (r, jnp.maximum(c - 1, 0))
     has_up = c < cols - 1
     has_down = c > 0
+    at_end = (c == 0) | (c == cols - 1)
+    inner = jnp.logical_not(at_end)
+    helper = (c == 1) | (c == cols - 2)
+    aided = jnp.where(c == 1, 0, cols - 1)
+    inward = jnp.where(c == 0, 1, cols - 2)
 
     barrier = pltpu.get_barrier_semaphore()
     for device in (right, left, partner):
@@ -157,19 +164,39 @@
     def beta_part(i, tile):
         return rowbuf[i].at[pl.ds(jnp.clip(tile, 0, cols - 1) * blocks_b, blocks_b)]
 
-    def beta_send(i, t):
+    def in_turn(i, tile, late):
+        if i < helped or helped == 0:
+            return jnp.bool_(not late) & (tile >= 0) & (tile < cols)
+        from_end = (tile == 0) | (tile == cols - 1)
+        return from_end if late else (tile > 0) & (tile < cols - 1)
+
+    def beta_send(i, t, late):
+        if late and (i < helped or helped == 0):
+            return
+        above = has_up & in_turn(i, c - t, late)
+        below = has_down & in_turn(i, c + t, late)
+        if i < helped:
+            above = above & (c + 1 < cols - 1)
+            below = below & (c - 1 > 0)
         ref = beta_part(i, c - t)
-        send(ref, ref, bsend.at[i, t], brecv.at[i, t], up, has_up & (c - t >= 0))
+        m = 2 * late * (cols - 1) + t
+        send(ref, ref, bsend.at[i, m], brecv.at[i, m], up, above)
         ref = beta_part(i, c + t)
-        m = cols - 1 + t
-        send(ref, ref, bsend.at[i, m], brecv.at[i, m], down, has_down & (c + t < cols))
-
-    def beta_arrive(i, t):
-        arrive(beta_part(i, c - 1 - t), bsend.at[i, t], brecv.at[i, t], c - 1 - t >= 0)
-        m = cols - 1 + t
-        arrive(beta_part(i, c + 1 + t), bsend.at[i, m], brecv.at[i, m], c + 1 + t < cols)
-
-    half = tables // 2
+        m = m + cols - 1
+        send(ref, ref, bsend.at[i, m], brecv.at[i, m], down, below)
+
+    def beta_arrive(i, t, late):
+        if late and (i < helped or helped == 0):
+            return
+        above = in_turn(i, c - 1 - t, late)
+        below = in_turn(i, c + 1 + t, late)
+        if i < helped:
+            above = above & inner
+            below = below & inner
+        m = 2 * late * (cols - 1) + t
+        arrive(beta_part(i, c - 1 - t), bsend.at[i, m], brecv.at[i, m], above)
+        m = m + cols - 1
+        arrive(beta_part(i, c + 1 + t), bsend.at[i, m], brecv.at[i, m], below)
 
     def table_places(s):
         source = c * spread + s
@@ -179,46 +206,86 @@
         distance = lax.rem(place - source_place + chips, chips)
         return lax.rem(source, 2), distance
 
-    def table_stage(s, first):
+    piece = tables // (2 * PIECES)
+
+    def table_stage(s, q, first):
         source_core, distance = table_places(s)
         mine = core == source_core
-        back = lax.rem(chips - distance, chips)
         at_source = mine & (distance == 0)
         for h in range(2):
-            ref = beta_tab.at[s, pl.ds(h * half, half)]
+            ref = beta_tab.at[s, pl.ds((h * PIECES + q) * piece, piece)]
             if first:
                 here = at_source
-                src = own_tab.at[pl.ds(h * half, half)]
+                src = own_tab.at[pl.ds((h * PIECES + q) * piece, piece)]
             else:
                 here = mine & (distance != 0)
                 src = ref
-                arrive(ref, tsend.at[s, h, 0], trecv.at[s, h], here)
-            limit = reach if h == 0 else reach - 1
-            other_limit = reach - 1 if h == 0 else reach
-            go_right = here & (distance + 1 <= limit)
-            go_left = here & (back + 1 <= other_limit)
-            base = 0 if first else 3
-            send(src, ref, tsend.at[s, h, base], trecv.at[s, h], right, go_right)
-            send(src, ref, tsend.at[s, h, base + 1], trecv.at[s, h], left, go_left)
-            send(src, ref, tsend.at[s, h, base + 2], trecv.at[s, h], partner, here)
+                arrive(ref, tsend.at[s, h, q, 0], trecv.at[s, h, q], here)
+            hops = distance if h == 0 else lax.rem(chips - distance, chips)
+            onward = here & (hops + 1 < chips)
+            base = 0 if first else 2
+            device = right if h == 0 else left
+            send(src, ref, tsend.at[s, h, q, base], trecv.at[s, h, q], device, onward)
+            send(src, ref, tsend.at[s, h, q, base + 1], trecv.at[s, h, q], partner, here)
 
     def table_finish(s):
         source_core, distance = table_places(s)
         mine = core == source_core
+        for q in range(PIECES):
+            for h in range(2):
+                ref = beta_tab.at[s, pl.ds((h * PIECES + q) * piece, piece)]
+                arrive(ref, tsend.at[s, h, q, 0], trecv.at[s, h, q], jnp.logical_not(mine))
+
+        @pl.when(mine & (distance == 0))
+        def _():
+            copy = pltpu.make_async_copy(own_tab, beta_tab.at[s], lsem.at[0])
+            copy.start()
+            copy.wait()
+
+    half = tables // 2
+
+    def help_send(s):
         for h in range(2):
-            ref = beta_tab.at[s, pl.ds(h * half, half)]
-            arrive(ref, tsend.at[s, h, 0], trecv.at[s, h], jnp.logical_not(mine))
-
+            ref = pl.ds(h * half, half)
+            send(beta_tab.at[s, ref], help_tab.at[s, ref], hsend.at[s, h, 0], hrecv.at[s, h],
+                 (r, inward), at_end & (core == s % 2))
+
+    def help_arrive(s):
+        for h in range(2):
+            ref = help_tab.at[s, pl.ds(h * half, half)]
+            arrive(ref, hsend.at[s, h, 1], hrecv.at[s, h], helper & (core == s % 2))
+            send(ref, ref, hsend.at[s, h, 1], hrecv.at[s, h], partner, helper & (core == s % 2))
+
+    def help_finish(s):
+        for h in range(2):
+            ref = help_tab.at[s, pl.ds(h * half, half)]
+            arrive(ref, hsend.at[s, h, 1], hrecv.at[s, h], helper & (core != s % 2))
+
+    def shared_part(i):
+        return shared.at[pl.ds(i * tall, tall)]
+
+    def widen(source, target):
+        for s in range(spread):
+            @pl.loop(0, tables)
+            def _(index):
+                signs = source[s, index, :size, :].astype(jnp.bfloat16)
+                target[s * tables + index] = jnp.concatenate([signs, signs], axis=1)
+
+    for s in range(spread):
+        for q in range(PIECES):
+            table_stage(s, q, True)
     for j in range(PARTS_A):
         alpha_send(j, 0)
         ref = colbuf[j].at[pl.ds(r * blocks, blocks)]
         send(ref, ref, asend.at[j, chips], arecv.at[j, chips], partner)
-        if j < PARTS_B:
-            beta_send(j, 0)
-    for i in range(PARTS_A, PARTS_B):
-        beta_send(i, 0)
-    for s in range(spread):
-        table_stage(s, True)
+        if j == 0:
+            for i in range(PARTS_B):
+                beta_send(i, 0, 0)
+            for q in range(PIECES):
+                for s in range(spread):
+                    table_stage(s, q, False)
+
+    out[...] = jnp.zeros_like(out)
 
     @pl.loop(0, tables)
     def _(index):
@@ -238,62 +305,100 @@
                 scale = own_tab[index, pl.ds(size, 1), :]
                 scale = jnp.concatenate([scale] * (wide // size), axis=1)
                 total = total + term * scale
-            out[pl.ds(pl.multiple_of(block * size, size), size), pl.ds(j * wide, wide)] = total
-
-    def beta_compute(i):
+            where = (pl.ds(pl.multiple_of(block * size, size), size), pl.ds(j * wide, wide))
+            out[where] = out[where] + total
+
+    def beta_compute(i, owner, tabs, signs, target, add):
         @pl.loop(0, blocks_b)
         def _(block):
             total = jnp.zeros((tall, size), jnp.float32)
             for l in range(link_max):
-                source = links[c * blocks_b + block, l]
+                source = links[owner * blocks_b + block, l]
                 high, low = split(rowbuf[i][source])
                 index = block * link_max + l
                 term = lax.dot_general(
-                    jnp.concatenate([high, low], axis=1), beta_signs[index],
+                    jnp.concatenate([high, low], axis=1), signs[index],
                     (((1,), (1,)), ((), ())), preferred_element_type=jnp.float32)
-                scale = beta_tab[block // blocks, lax.rem(index, tables), pl.ds(size, 1), :]
+                scale = tabs[block // blocks, lax.rem(index, tables), pl.ds(size, 1), :]
                 total = total + term * scale
             where = (pl.ds(i * tall, tall), pl.ds(pl.multiple_of(block * size, size), size))
-            out[where] = out[where] + total
-
-    for t in range(1, max(reach, cols - 1) + 1):
-        for j in range(max(PARTS_A, PARTS_B)):
-            if j < PARTS_A and t <= reach:
-                alpha_arrive(j, t - 1)
-                if t < reach:
-                    alpha_send(j, t)
-            if j < PARTS_B and t < cols - 1:
-                beta_arrive(j, t - 1)
-                beta_send(j, t)
-            if t == 1 and j == PARTS_A - 1:
-                for s in range(spread):
-                    table_stage(s, False)
-            if t == reach and j < PARTS_A:
-                if j > 0:
-                    alpha_partner(j - 1)
-                    alpha_compute(j - 1)
-        if t == reach:
-            alpha_partner(PARTS_A - 1)
-            alpha_compute(PARTS_A - 1)
-            for s in range(spread):
-                source_core, distance = table_places(s)
-
-                @pl.when((core == source_core) & (distance == 0))
-                def _():
-                    copy = pltpu.make_async_copy(own_tab, beta_tab.at[s], lsem.at[0])
-                    copy.start()
-                    copy.wait()
-
-                table_finish(s)
-
-                @pl.loop(0, tables)
-                def _(index):
-                    signs = beta_tab[s, index, :size, :].astype(jnp.bfloat16)
-                    beta_signs[s * tables + index] = jnp.concatenate([signs, signs], axis=1)
-
+            if add:
+                total = target[where] + total
+            target[where] = total
+
+    for s in range(spread):
+        table_finish(s)
+    if helped:
+        for s in range(spread):
+            help_send(s)
     for i in range(PARTS_B):
-        beta_arrive(i, cols - 2)
-        beta_compute(i)
+        beta_send(i, 0, 1)
+    widen(beta_tab, beta_signs)
+
+    for t in range(cols - 1):
+        for i in range(PARTS_B):
+            beta_arrive(i, t, 0)
+            if t < cols - 2:
+                beta_send(i, t + 1, 0)
+        if t < reach - 1:
+            for j in range(PARTS_A):
+                alpha_arrive(j, t)
+                alpha_send(j, t + 1)
+    for t in range(cols - 1, reach - 1):
+        for j in range(PARTS_A):
+            alpha_arrive(j, t)
+            alpha_send(j, t + 1)
+
+    def own_helped(add):
+        for i in range(helped):
+            @pl.when(inner)
+            def _():
+                beta_compute(i, c, beta_tab, beta_signs, out, add)
+
+    own_helped(True)
+    if helped:
+        for s in range(spread):
+            help_arrive(s)
+        for s in range(spread):
+            help_finish(s)
+
+        @pl.when(helper)
+        def _():
+            widen(help_tab, help_signs)
+
+        for i in range(helped):
+            @pl.when(helper)
+            def _():
+                beta_compute(i, aided, help_tab, help_signs, shared, False)
+
+            send(shared_part(i), shared_part(i), rsend.at[i], rrecv.at[i], (r, aided), helper)
+
+    for j in range(PARTS_A):
+        alpha_arrive(j, reach - 1)
+        alpha_partner(j)
+        if j % 2 == 0:
+            i = helped + j // 2
+            if i < PARTS_B:
+                beta_arrive(i, 0, 1)
+                beta_send(i, 1, 1)
+        alpha_compute(j)
+    for i in range(helped + (PARTS_A + 1) // 2, PARTS_B):
+        beta_arrive(i, 0, 1)
+        beta_send(i, 1, 1)
+    for i in range(helped):
+        arrive(shared_part(i), rsend.at[i], rrecv.at[i], at_end)
+
+        @pl.when(at_end)
+        def _():
+            rows_here = pl.ds(i * tall, tall)
+            out[rows_here, :] = out[rows_here, :] + shared[rows_here, :]
+
+    for i in range(helped, PARTS_B):
+        for t in range(1, cols - 2):
+            beta_arrive(i, t, 1)
+            beta_send(i, t + 1, 1)
+        beta_arrive(i, cols - 2, 1)
+        beta_compute(i, c, beta_tab, beta_signs, out, True)
 
     for cond, copy in pending:
         if cond is None:
@@ -319,14 +424,21 @@
     scratch += [
         pltpu.VMEM((tables, size + PAD, size), jnp.float32),
         pltpu.VMEM((spread, tables, size + PAD, size), jnp.float32),
+        pltpu.VMEM((spread, tables, size + PAD, size), jnp.float32),
         pltpu.VMEM((tables, size, 2 * size), jnp.bfloat16),
         pltpu.VMEM((spread * tables, size, 2 * size), jnp.bfloat16),
+        pltpu.VMEM((spread * tables, size, 2 * size), jnp.bfloat16),
+        pltpu.VMEM((high // 2, width), jnp.float32),
         pltpu.SemaphoreType.DMA((PARTS_A, 2 * chips + 1)),
         pltpu.SemaphoreType.DMA((PARTS_A, 2 * chips + 1)),
-        pltpu.SemaphoreType.DMA((PARTS_B, 2 * cols - 2)),
-        pltpu.SemaphoreType.DMA((PARTS_B, 2 * cols - 2)),
-        pltpu.SemaphoreType.DMA((spread, 2, 6)),
+        pltpu.SemaphoreType.DMA((PARTS_B, 4 * cols - 4)),
+        pltpu.SemaphoreType.DMA((PARTS_B, 4 * cols - 4)),
+        pltpu.SemaphoreType.DMA((spread, 2, PIECES, 4)),
+        pltpu.SemaphoreType.DMA((spread, 2, PIECES)),
+        pltpu.SemaphoreType.DMA((spread, 2, 2)),
         pltpu.SemaphoreType.DMA((spread, 2)),
+        pltpu.SemaphoreType.DMA((PARTS_B,)),
+        pltpu.SemaphoreType.DMA((PARTS_B,)),
         pltpu.SemaphoreType.DMA((PARTS_A * blocks + PARTS_B * blocks * spread + 1,)),
     ]
     return pl.pallas_call(

time: 184 us -> 238 us (1.29)
  Pallas kernels: 174 us -> 226 us
    pallas_call x1, Pallas kernels: 174 us -> 226 us  [local(): pl.pallas_call(functools.partial(kernel, rows, cols, blocks, link_max), o...]
where the time goes in v2:
time: 238 us; the launch traced here: 236 us
  Pallas kernels  226 us (95%)
  local copies, waits for them, and re-layouts  5.53 us (2%)
  other arithmetic  4.21 us (2%)
    pallas_call x1, Pallas kernels, local(): pl.pallas_call(functools.partial(kernel, rows, cols, blocks, link_max), o...  226 us

profile of v2, /device:TPU:4, one launch (start us, length us, event | category | flops | bytes accessed | tf_op | source)
XLA Modules:
  0.0 236.0 jit_solution(12778652503211799481)
XLA Ops:
  0.0 0.7 dynamic_slice.3
  0.7 0.8 broadcast_in_dim.27
  1.5 0.8 select_reduce_fusion
  2.3 0.1 fusion
  2.4 0.1 select_n.21
  2.5 0.1 broadcast_in_dim.31
  2.6 1.7 convert_element_type.6
  4.3 0.0 copy-start
  4.4 1.6 pad_maximum_fusion.tab
  5.9 0.0 copy-done
  5.9 0.7 copy.8.links
  6.6 226.2 %shard_map.64 = f32[512,1024]{1,0:T(8,128)} custom-call(s32[32,8]{1,0:T(8,128)} %copy.8.links, f32[512,1024]{1,0:T(8,128)} %v.1, f32[32,136,128]{2,1,0:T(8,128)} %pad_maximum_fusion.tab), custom_call_target="tpu_custom_call" | custom-call | tf_op jit(solution)/shard_map/pallas_call | solution.py:444
  232.8 3.2 %copy.10 = f32[512,1024]{1,0:T(8,128)} copy(f32[512,1024]{1,0:T(8,128)} %shard_map.64) | data formatting | bytes 4194304
Async XLA Ops:
  4.3 1.6 copy-start

commit v3 on v2

--- a/solution.py
+++ b/solution.py
@@ -208,25 +208,20 @@
 
     piece = tables // (2 * PIECES)
 
-    def table_stage(s, q, first):
+    def table_stage(s, q, d):
         source_core, distance = table_places(s)
-        mine = core == source_core
-        at_source = mine & (distance == 0)
         for h in range(2):
-            ref = beta_tab.at[s, pl.ds((h * PIECES + q) * piece, piece)]
-            if first:
-                here = at_source
-                src = own_tab.at[pl.ds((h * PIECES + q) * piece, piece)]
-            else:
-                here = mine & (distance != 0)
-                src = ref
+            hops = distance if h == 0 else lax.rem(chips - distance, chips)
+            here = (core == source_core) & (hops == d)
+            part = pl.ds((h * PIECES + q) * piece, piece)
+            ref = beta_tab.at[s, part]
+            src = ref if d else own_tab.at[part]
+            if d:
                 arrive(ref, tsend.at[s, h, q, 0], trecv.at[s, h, q], here)
-            hops = distance if h == 0 else lax.rem(chips - distance, chips)
-            onward = here & (hops + 1 < chips)
-            base = 0 if first else 2
-            device = right if h == 0 else left
-            send(src, ref, tsend.at[s, h, q, base], trecv.at[s, h, q], device, onward)
-            send(src, ref, tsend.at[s, h, q, base + 1], trecv.at[s, h, q], partner, here)
+            if d + 1 < chips:
+                send(src, ref, tsend.at[s, h, q, 0], trecv.at[s, h, q],
+                     right if h == 0 else left, here)
+            send(src, ref, tsend.at[s, h, q, 1], trecv.at[s, h, q], partner, here)
 
     def table_finish(s):
         source_core, distance = table_places(s)
@@ -273,7 +268,7 @@
 
     for s in range(spread):
         for q in range(PIECES):
-            table_stage(s, q, True)
+            table_stage(s, q, 0)
     for j in range(PARTS_A):
         alpha_send(j, 0)
         ref = colbuf[j].at[pl.ds(r * blocks, blocks)]
@@ -281,9 +276,11 @@
         if j == 0:
             for i in range(PARTS_B):
                 beta_send(i, 0, 0)
-            for q in range(PIECES):
-                for s in range(spread):
-                    table_stage(s, q, False)
+            for wave in range(PIECES + chips - 2):
+                for q in range(PIECES):
+                    if 1 <= wave - q + 1 < chips:
+                        for s in range(spread):
+                            table_stage(s, q, wave - q + 1)
 
     out[...] = jnp.zeros_like(out)
 
@@ -433,7 +430,7 @@
         pltpu.SemaphoreType.DMA((PARTS_A, 2 * chips + 1)),
         pltpu.SemaphoreType.DMA((PARTS_B, 4 * cols - 4)),
         pltpu.SemaphoreType.DMA((PARTS_B, 4 * cols - 4)),
-        pltpu.SemaphoreType.DMA((spread, 2, PIECES, 4)),
+        pltpu.SemaphoreType.DMA((spread, 2, PIECES, 2)),
         pltpu.SemaphoreType.DMA((spread, 2, PIECES)),
         pltpu.SemaphoreType.DMA((spread, 2, 2)),
         pltpu.SemaphoreType.DMA((spread, 2)),

time: 238 us -> 171 us (0.72)
  Pallas kernels: 226 us -> 161 us
    pallas_call x1, Pallas kernels: 226 us -> 161 us  [local(): pl.pallas_call(functools.partial(kernel, rows, cols, blocks, link_max), o...]
where the time goes in v3:
time: 171 us
  Pallas kernels  161 us (94%)
  local copies, waits for them, and re-layouts  5.53 us (3%)
  other arithmetic  4.21 us (2%)
    pallas_call x1, Pallas kernels, local(): pl.pallas_call(functools.partial(kernel, rows, cols, blocks, link_max), o...  161 us
    unnamed x4, local copies, waits for them, and re-layouts  3.85 us

profile of v3, /device:TPU:4, one launch (start us, length us, event | category | flops | bytes accessed | tf_op | source)
XLA Modules:
  0.0 170.5 jit_solution(12608350670377188102)
XLA Ops:
  0.0 0.7 dynamic_slice.3
  0.7 0.8 broadcast_in_dim.27
  1.5 0.8 select_reduce_fusion
  2.3 0.1 fusion
  2.4 0.1 select_n.21
  2.5 0.1 broadcast_in_dim.31
  2.6 1.7 %convert_element_type.6 = f32[4,8,128,128]{3,2,1,0:T(8,128)S(1)} convert(s32[4,8,128,128]{3,2,1,0:T(8,128)} %param.11) | non-fusion elementwise | flops 524288 | bytes 4194304 | tf_op jit(solution)/shard_map/convert_element_type | solution.py:416
  4.3 0.0 copy-start
  4.4 1.6 pad_maximum_fusion.tab
  5.9 0.0 copy-done
  5.9 0.7 copy.8.links
  6.6 160.8 %shard_map.64 = f32[512,1024]{1,0:T(8,128)} custom-call(s32[32,8]{1,0:T(8,128)} %copy.8.links, f32[512,1024]{1,0:T(8,128)} %v.1, f32[32,136,128]{2,1,0:T(8,128)} %pad_maximum_fusion.tab), custom_call_target="tpu_custom_call" | custom-call | tf_op jit(solution)/shard_map/pallas_call | solution.py:441
  167.4 3.2 %copy.10 = f32[512,1024]{1,0:T(8,128)} copy(f32[512,1024]{1,0:T(8,128)} %shard_map.64) | data formatting | bytes 4194304
Async XLA Ops:
  4.3 1.6 copy-start

commit v4 on v3

--- a/solution.py
+++ b/solution.py
@@ -276,6 +276,7 @@
         if j == 0:
             for i in range(PARTS_B):
                 beta_send(i, 0, 0)
+                beta_send(i, 0, 1)
             for wave in range(PIECES + chips - 2):
                 for q in range(PIECES):
                     if 1 <= wave - q + 1 < chips:
@@ -328,8 +329,6 @@
     if helped:
         for s in range(spread):
             help_send(s)
-    for i in range(PARTS_B):
-        beta_send(i, 0, 1)
     widen(beta_tab, beta_signs)
 
     for t in range(cols - 1):
@@ -352,7 +351,14 @@
             def _():
                 beta_compute(i, c, beta_tab, beta_signs, out, add)
 
+    for i in range(helped, PARTS_B):
+        beta_arrive(i, 0, 1)
+        beta_send(i, 1, 1)
     own_helped(True)
+    for t in range(1, cols - 2):
+        for i in range(helped, PARTS_B):
+            beta_arrive(i, t, 1)
+            beta_send(i, t + 1, 1)
     if helped:
         for s in range(spread):
             help_arrive(s)
@@ -373,15 +379,7 @@
     for j in range(PARTS_A):
         alpha_arrive(j, reach - 1)
         alpha_partner(j)
-        if j % 2 == 0:
-            i = helped + j // 2
-            if i < PARTS_B:
-                beta_arrive(i, 0, 1)
-                beta_send(i, 1, 1)
         alpha_compute(j)
-    for i in range(helped + (PARTS_A + 1) // 2, PARTS_B):
-        beta_arrive(i, 0, 1)
-        beta_send(i, 1, 1)
     for i in range(helped):
         arrive(shared_part(i), rsend.at[i], rrecv.at[i], at_end)
 
@@ -391,9 +389,6 @@
             out[rows_here, :] = out[rows_here, :] + shared[rows_here, :]
 
     for i in range(helped, PARTS_B):
-        for t in range(1, cols - 2):
-            beta_arrive(i, t, 1)
-            beta_send(i, t + 1, 1)
         beta_arrive(i, cols - 2, 1)
         beta_compute(i, c, beta_tab, beta_signs, out, True)
 

time: 171 us -> 160 us (0.936)
  the two profiles are of different devices: /device:TPU:4 before, /device:TPU:0 now
where the time goes in v4:
time: 160 us; the launch traced here: 159 us
  Pallas kernels  150 us (94%)
  local copies, waits for them, and re-layouts  5.53 us (3%)
  other arithmetic  4.21 us (3%)
    pallas_call x1, Pallas kernels, local(): pl.pallas_call(functools.partial(kernel, rows, cols, blocks, link_max), o...  150 us
    unnamed x4, local copies, waits for them, and re-layouts  3.85 us

profile of v4, /device:TPU:0, one launch (start us, length us, event | category | flops | bytes accessed | tf_op | source)
XLA Modules:
  0.0 159.5 jit_solution(11074984708017093249)
XLA Ops:
  0.0 0.7 dynamic_slice.3
  0.7 0.8 broadcast_in_dim.27
  1.5 0.8 select_reduce_fusion
  2.3 0.1 fusion
  2.4 0.1 select_n.21
  2.5 0.1 broadcast_in_dim.31
  2.6 1.7 %convert_element_type.6 = f32[4,8,128,128]{3,2,1,0:T(8,128)S(1)} convert(s32[4,8,128,128]{3,2,1,0:T(8,128)} %param.11) | non-fusion elementwise | flops 524288 | bytes 4194304 | tf_op jit(solution)/shard_map/convert_element_type | solution.py:411
  4.3 0.0 copy-start
  4.4 1.6 pad_maximum_fusion.tab
  5.9 0.0 copy-done
  5.9 0.7 copy.8.links
  6.6 149.7 %shard_map.64 = f32[512,1024]{1,0:T(8,128)} custom-call(s32[32,8]{1,0:T(8,128)} %copy.8.links, f32[512,1024]{1,0:T(8,128)} %v.1, f32[32,136,128]{2,1,0:T(8,128)} %pad_maximum_fusion.tab), custom_call_target="tpu_custom_call" | custom-call | tf_op jit(solution)/shard_map/pallas_call | solution.py:436
  156.3 3.2 %copy.10 = f32[512,1024]{1,0:T(8,128)} copy(f32[512,1024]{1,0:T(8,128)} %shard_map.64) | data formatting | bytes 4194304
Async XLA Ops:
  4.3 1.6 copy-start
